TPU v7x, 256 devices: a whole 4x4x8 slice. The times are simulated.
256 devices in a mesh: gx: 8 (over x, core), gy: 4 (over z_lo), gz: 8 (over y, z_hi).
Axes of the slice: x: 4, y: 4, z: 8 (z_hi: 2, z_lo: 4; z = z_hi * 4 + z_lo), core: 2. Of those that a mesh axis runs over, the one named last changes fastest.
Arguments:
- start_block: float32 [32, 3, 2, 8, 16, 1024], P(None, None, None, 'gx', 'gy', 'gz'), may hold values from -700 to 700
- pair_blocks: float32 [3, 3, 16, 2, 8, 16, 1024], P(None, None, None, None, 'gx', 'gy', 'gz'), may hold values from -8 to 8, as said below
- slot_map: int32 [16, 2, 8, 16, 1024], P(None, None, 'gx', 'gy', 'gz'), may hold values from 0 to 15, as said below
Outputs:
- alpha1: float32 [32, 32], replicated
- alpha2: float32 [32, 32], replicated
- beta1: float32 [32, 32], replicated
- beta2: float32 [32, 32], replicated
- basis3: float32 [32, 3, 2, 8, 16, 1024], P(None, None, None, 'gx', 'gy', 'gz')
Inputs may be any that keep to these rules, and one draw needn't show every extreme that they name: `slot_map`: for every atom the 16 slots hold each of 0 to 15 once; 0 to 13 name the neighbour directions of the steps, 14 and 15 mark padding slots. `pair_blocks`: the block an atom holds toward a neighbour is the transpose of the block that neighbour holds toward the atom, so H is symmetric.
All inputs are finite; a program needn't handle non-finite values.
Results may differ from a plain program's by a relative error of at most 0.0003.
Values sent between devices are 32-bit elements; how exact they have to be, the bound alone decides.
A program may use at most 64 MiB of HBM per device.

v0:
```python
import jax
import jax.numpy as jnp
from jax import lax
from jax.sharding import PartitionSpec as P

PRECISE = lax.Precision.HIGHEST


def extended(block, sides, width):
    for axis, dim in sides:
        count = lax.axis_size(axis)
        forward = [(i, i + 1) for i in range(count - 1)]
        forward.append((count - 1, 0))
        backward = [(target, source) for source, target in forward]
        low = lax.ppermute(
            lax.slice_in_dim(block, block.shape[dim] - width, None, axis=dim), axis, forward
        )
        high = lax.ppermute(lax.slice_in_dim(block, 0, width, axis=dim), axis, backward)
        block = jnp.concatenate([low, block, high], axis=dim)
    return block


def neighbour_offset(sublattice, offset_id):
    if offset_id < 8:
        corner_bits = (offset_id >> 2 & 1, offset_id >> 1 & 1, offset_id & 1)
        if sublattice == 0:
            return ((-corner_bits[0], -corner_bits[1], -corner_bits[2]), 1)
        return (corner_bits, 0)
    axis_id = (offset_id - 8) // 2
    direction = 1 if (offset_id - 8) % 2 == 0 else -1
    displacement = tuple((direction if axis_number == axis_id else 0 for axis_number in range(3)))
    return (displacement, sublattice)


def offset_blocks(pair_blocks, slot_map):
    result = []
    for offset_id in range(14):
        chosen = slot_map[None, None] == offset_id
        result.append(jnp.sum(jnp.where(chosen, pair_blocks, jnp.float32(0.0)), axis=2))
    return result


def onsite_blocks(blocks):
    result = []
    for sublattice in range(2):
        onsite = jnp.zeros(blocks[0].shape[:2] + blocks[0].shape[3:], jnp.float32)
        for offset_id in range(14):
            coupling = blocks[offset_id][:, :, sublattice]
            onsite = onsite + 0.5 * (coupling + jnp.swapaxes(coupling, 0, 1))
        result.append(onsite)
    return result


def apply_hessian(vectors, blocks, onsite):
    padded = extended(vectors, (("gx", 3), ("gy", 4), ("gz", 5)), 1)
    size_x, size_y, size_z = (vectors.shape[3], vectors.shape[4], vectors.shape[5])
    outputs = []
    for sublattice in range(2):
        summed = jnp.zeros(vectors.shape[:2] + vectors.shape[3:], jnp.float32)
        for offset_id in range(14):
            displacement, source = neighbour_offset(sublattice, offset_id)
            start_x = 1 + displacement[0]
            start_y = 1 + displacement[1]
            start_z = 1 + displacement[2]
            neighbour = padded[
                :,
                :,
                source,
                start_x : start_x + size_x,
                start_y : start_y + size_y,
                start_z : start_z + size_z,
            ]
            coupling = blocks[offset_id][:, :, sublattice]
            summed = summed + jnp.sum(coupling[None] * neighbour[:, None], axis=2)
        summed = summed - jnp.sum(
            onsite[sublattice][None] * vectors[:, None, :, sublattice], axis=2
        )
        outputs.append(summed)
    return jnp.stack(outputs, axis=2)


def local_gram(left, right):
    left_flat = left.reshape(left.shape[0], -1)
    right_flat = right.reshape(right.shape[0], -1)
    return lax.dot_general(left_flat, right_flat, (((1,), (1,)), ((), ())), precision=PRECISE)


def combine(matrix, vectors):
    flat = vectors.reshape(vectors.shape[0], -1)
    return jnp.dot(matrix, flat, precision=PRECISE).reshape(vectors.shape)


def inverse_factor(gram_matrix):
    lower = jnp.linalg.cholesky(gram_matrix)
    identity = jnp.eye(gram_matrix.shape[0], dtype=gram_matrix.dtype)
    inverse = jax.scipy.linalg.solve_triangular(lower, identity, lower=True)
    return (lower, inverse)


def lanczos_step(basis, image, previous, coupling_prev, row_count):
    alpha = lax.psum(local_gram(image, basis), ("gx", "gy", "gz")) / row_count
    residual = image - combine(alpha, basis)
    if previous is not None:
        residual = residual - combine(coupling_prev.T, previous)
    residual_gram = lax.psum(local_gram(residual, residual), ("gx", "gy", "gz")) / row_count
    return (alpha, residual, residual_gram)


def local(start_block, pair_blocks, slot_map):
    device_count = lax.axis_size("gx") * lax.axis_size("gy") * lax.axis_size("gz")
    row_count = start_block[0].size * device_count
    blocks = offset_blocks(pair_blocks, slot_map)
    onsite = onsite_blocks(blocks)
    start_gram = lax.psum(local_gram(start_block, start_block), ("gx", "gy", "gz")) / row_count
    lower0, inverse0 = inverse_factor(start_gram)
    basis1 = combine(inverse0, start_block)
    image1 = apply_hessian(basis1, blocks, onsite)
    alpha1, residual1, gram_first = lanczos_step(basis1, image1, None, None, row_count)
    beta1, inverse1 = inverse_factor(gram_first)
    basis2 = combine(inverse1, residual1)
    image2 = apply_hessian(basis2, blocks, onsite)
    alpha2, residual2, gram_second = lanczos_step(basis2, image2, basis1, beta1, row_count)
    beta2, inverse2 = inverse_factor(gram_second)
    basis3 = combine(inverse2, residual2)
    return (alpha1, alpha2, beta1, beta2, basis3)


def solution(mesh):
    in_specs = (
        P(None, None, None, "gx", "gy", "gz"),
        P(None, None, None, None, "gx", "gy", "gz"),
        P(None, None, "gx", "gy", "gz"),
    )
    out_specs = (P(), P(), P(), P(), P(None, None, None, "gx", "gy", "gz"))
    return jax.shard_map(local, mesh=mesh, in_specs=in_specs, out_specs=out_specs, check_vma=False)
```

profile of v0, /device:TPU:1, one launch (start us, length us, event | category | flops | bytes accessed | tf_op | source)
XLA Modules:
  0.0 522.5 jit_solution(3226206658296597986)
XLA Ops:
  0.6 1.2 reshape.1549
  1.8 1.6 convolution_bitcast_fusion.2
  3.4 81.5 %psum.35 = f32[32,32]{0,1:T(8,128)S(1)} all-reduce(f32[32,32]{0,1:T(8,128)S(1)} %convolution_bitcast_fusion.2), channel_id=1, replica_groups=mesh['gx'=8,'gy'=4,'gz'=8] {'gx','gy','gz'}, use_global_device_ids=true, to_apply=%region_1.2 | all-reduce | flops 1024 | bytes 8192 | tf_op jit(solution)/shard_map/psum | solution.py:114
  85.0 2.9 cholesky.59
  88.6 0.7 fusion.44
  89.3 2.4 custom-call.7
  92.8 1.0 collective-permute-start.1
  94.1 2.5 select_reduce_fusion.13
  103.9 0.8 multiply_reduce_fusion.45
  104.7 0.8 multiply_reduce_fusion.59
  106.4 2.7 collective-permute-start.3
  109.2 0.7 slice_bitcast_fusion.9
  109.9 0.7 multiply_reduce_fusion.50
  110.6 0.9 multiply_reduce_fusion.55
  111.5 0.9 multiply_reduce_fusion.51
  112.3 1.1 collective-permute-done.2
  113.4 6.9 %collective-permute-done.3 = f32[32,3,2,3,1,128]{5,0,4,3,2,1:T(8,128)S(1)} collective-permute-done((f32[32,3,2,3,1,128]{5,0,4,3,2,1:T(8,128)S(1)}, f32[32,3,2,3,1,128]{5,0,4,3,2,1:T(8,128)S(1)}, u32[]{:S(2)}, u32[]{:S(2)}) %collective-permute-start.3) | collective-permute-done | bytes 294944 | tf_op jit(solution)/shard_map/ppermute | solution.py:18
  120.3 0.7 copy-done.10
  121.2 1.8 fusion.52
  123.1 2.8 copy.507
  125.9 5.6 %collective-permute-start.5 = (f32[32,3,2,3,6,1]{0,2,5,4,3,1:T(2,128)}, f32[32,3,2,3,6,1]{0,2,5,4,3,1:T(2,128)}, u32[]{:S(2)}, u32[]{:S(2)}) collective-permute-start(f32[32,3,2,3,6,1]{0,2,5,4,3,1:T(2,128)} %copy.507), channel_id=1, source_target_pairs={{1,0},{2,1},{3,2},{4,3},{5,4},{6,5},{7,6},{0,7},{9,8},{10,9},{11,1... | collective-permute-start | bytes 41480 | tf_op jit(solution)/shard_map/ppermute | solution.py:18
  131.5 1.3 copy.506
  132.8 1.7 multiply_reduce_fusion.36
  134.5 2.7 copy.419
  137.2 5.0 collective-permute-done.4
  142.2 1.5 copy.395
  143.8 1.4 fusion.8
  151.0 74.3 %psum.36 = f32[32,32]{0,1:T(8,128)S(1)} all-reduce(f32[32,32]{0,1:T(8,128)S(1)} %fusion.56), channel_id=1, replica_groups=mesh['gx'=8,'gy'=4,'gz'=8] {'gx','gy','gz'}, use_global_device_ids=true, to_apply=%region_47.50 | all-reduce | flops 1024 | bytes 8192 | tf_op jit(solution)/shard_map/psum | solution.py:101
  226.4 73.7 %psum.37 = f32[32,32]{0,1:T(8,128)S(1)} all-reduce(f32[32,32]{0,1:T(8,128)S(1)} %fusion.57), channel_id=1, replica_groups=mesh['gx'=8,'gy'=4,'gz'=8] {'gx','gy','gz'}, use_global_device_ids=true, to_apply=%region_48.51 | all-reduce | flops 1024 | bytes 8192 | tf_op jit(solution)/shard_map/psum | solution.py:105
  300.2 2.9 cholesky.70
  304.4 2.4 custom-call.8
  307.9 1.2 collective-permute-start.6
  309.2 0.8 multiply_reduce_fusion.15
  310.1 0.8 multiply_reduce_fusion.29
  311.0 0.7 copy.495
  311.7 2.2 collective-permute-done.6
  314.0 2.6 collective-permute-done.7
  316.7 1.0 collective-permute-start.8
  317.7 2.4 collective-permute-start.9
  320.2 0.7 multiply_reduce_fusion.20
  320.9 0.9 multiply_reduce_fusion.25
  321.8 0.9 multiply_reduce_fusion.21
  322.6 4.1 collective-permute-done.8
  326.7 5.3 %collective-permute-done.9 = f32[32,3,2,3,1,128]{5,0,4,3,2,1:T(8,128)S(1)} collective-permute-done((f32[32,3,2,3,1,128]{5,0,4,3,2,1:T(8,128)S(1)}, f32[32,3,2,3,1,128]{5,0,4,3,2,1:T(8,128)S(1)}, u32[]{:S(2)}, u32[]{:S(2)}) %collective-permute-start.9) | collective-permute-done | bytes 294944 | tf_op jit(solution)/shard_map/ppermute | solution.py:18
  332.0 0.7 copy-done.6
  332.9 1.8 fusion.51
  334.8 2.8 copy.509
  337.6 4.7 collective-permute-start.11
  342.2 1.5 multiply_reduce_fusion.6
  343.7 1.3 copy.508
  345.0 0.7 collective-permute-start.10
  345.7 1.5 copy.488
  347.2 2.2 maximum_bitcast_fusion.4
  349.5 0.9 multiply_reduce_fusion.17
  350.4 4.6 collective-permute-done.10
  354.9 1.5 copy.486
  356.5 1.4 fusion.4
  363.7 73.7 %psum.38 = f32[32,32]{0,1:T(8,128)S(1)} all-reduce(f32[32,32]{0,1:T(8,128)S(1)} %fusion.59), channel_id=1, replica_groups=mesh['gx'=8,'gy'=4,'gz'=8] {'gx','gy','gz'}, use_global_device_ids=true, to_apply=%region_79.82 | all-reduce | flops 1024 | bytes 8192 | tf_op jit(solution)/shard_map/psum | solution.py:101
  439.1 73.7 %psum.39 = f32[32,32]{0,1:T(8,128)S(1)} all-reduce(f32[32,32]{0,1:T(8,128)S(1)} %fusion.60), channel_id=1, replica_groups=mesh['gx'=8,'gy'=4,'gz'=8] {'gx','gy','gz'}, use_global_device_ids=true, to_apply=%region_80.83 | all-reduce | flops 1024 | bytes 8192 | tf_op jit(solution)/shard_map/psum | solution.py:105
  512.8 2.9 cholesky.81
  516.4 1.3 select_bitcast_fusion
  517.6 2.4 custom-call.9
  520.8 1.0 copy.497
  521.8 0.7 copy.496
  (321 shorter events, 28.2 us)
Async XLA Ops:
  3.4 90.4 %copy-start.95 = (s32[16,2,1,4,128]{4,3,2,1,0:T(4,128)S(1)}, s32[16,2,1,4,128]{4,3,2,1,0:T(4,128)}, u32[]{:S(2)}) copy-start(s32[16,2,1,4,128]{4,3,2,1,0:T(4,128)} %param.8) | copy-start | bytes 196612
  88.6 5.5 %copy-start.35 = (f32[3,3,16,2,1,4,128]{6,5,4,3,2,1,0:T(4,128)S(1)}, f32[3,3,16,2,1,4,128]{6,5,4,3,2,1,0:T(4,128)}, u32[]{:S(2)}) copy-start(f32[3,3,16,2,1,4,128]{6,5,4,3,2,1,0:T(4,128)} %param.7) | copy-start | bytes 1769476
  92.8 12.8 %collective-permute-start = (f32[32,3,2,1,4,128]{5,0,4,3,2,1:T(8,128)S(1)}, f32[32,3,2,1,4,128]{5,0,4,3,2,1:T(8,128)S(1)}, u32[]{:S(2)}, u32[]{:S(2)}) collective-permute-start(f32[32,3,2,1,4,128]{5,0,4,3,2,1:T(8,128)S(1)} %copy.391), channel_id=1, source_target_pairs={{0,32},{32,64},{64,96},{96,128},{128,160},{160,192},{192,224},{224... | collective-permute-start | bytes 1179656 | tf_op jit(solution)/shard_map/ppermute | solution.py:15
  92.8 12.9 %collective-permute-start.1 = (f32[32,3,2,1,4,128]{5,0,4,3,2,1:T(8,128)S(1)}, f32[32,3,2,1,4,128]{5,0,4,3,2,1:T(8,128)S(1)}, u32[]{:S(2)}, u32[]{:S(2)}) collective-permute-start(f32[32,3,2,1,4,128]{5,0,4,3,2,1:T(8,128)S(1)} %copy.391), channel_id=1, source_target_pairs={{32,0},{64,32},{96,64},{128,96},{160,128},{192,160},{224,192},{0,2... | collective-permute-start | bytes 1179656 | tf_op jit(solution)/shard_map/ppermute | solution.py:18
  99.9 10.0 %copy-start.84 = (f32[3,3,4,128]{3,2,0,1:T(4,128)}, f32[3,3,4,128]{3,2,0,1:T(4,128)S(1)}, u32[]{:S(2)}) copy-start(f32[3,3,4,128]{3,2,0,1:T(4,128)S(1)} %get-tuple-element.159) | copy-start | bytes 55300
  99.9 10.7 %copy-start.82 = (f32[3,3,4,128]{3,2,0,1:T(4,128)}, f32[3,3,4,128]{3,2,0,1:T(4,128)S(1)}, u32[]{:S(2)}) copy-start(f32[3,3,4,128]{3,2,0,1:T(4,128)S(1)} %get-tuple-element.162) | copy-start | bytes 55300
  100.5 10.9 %copy-start.80 = (f32[3,3,4,128]{3,2,0,1:T(4,128)}, f32[3,3,4,128]{3,2,0,1:T(4,128)S(1)}, u32[]{:S(2)}) copy-start(f32[3,3,4,128]{3,2,0,1:T(4,128)S(1)} %get-tuple-element.194) | copy-start | bytes 55300
  102.5 8.1 %copy-start.88 = (f32[3,3,4,128]{3,2,0,1:T(4,128)}, f32[3,3,4,128]{3,2,0,1:T(4,128)S(1)}, u32[]{:S(2)}) copy-start(f32[3,3,4,128]{3,2,0,1:T(4,128)S(1)} %get-tuple-element.190) | copy-start | bytes 55300
  102.5 9.0 %copy-start.86 = (f32[3,3,4,128]{3,2,0,1:T(4,128)}, f32[3,3,4,128]{3,2,0,1:T(4,128)S(1)}, u32[]{:S(2)}) copy-start(f32[3,3,4,128]{3,2,0,1:T(4,128)S(1)} %get-tuple-element.189) | copy-start | bytes 55300
  103.8 1.8 copy-start.90
  103.8 1.8 copy-start.92
  103.9 1.9 copy-start.36
  104.7 1.1 copy-start.38
  105.8 7.6 %collective-permute-start.2 = (f32[32,3,2,3,1,128]{5,0,4,3,2,1:T(8,128)S(1)}, f32[32,3,2,3,1,128]{5,0,4,3,2,1:T(8,128)S(1)}, u32[]{:S(2)}, u32[]{:S(2)}) collective-permute-start(f32[32,3,2,3,1,128]{5,0,4,3,2,1:T(8,128)S(1)} %get-tuple-element.115), channel_id=1, source_target_pairs={{0,8},{8,16},{16,24},{24,0},{1,9},{9,17},{17,25},{25,1},{2,10},{10... | collective-permute-start | bytes 884744 | tf_op jit(solution)/shard_map/ppermute | solution.py:15
  106.4 13.9 %collective-permute-start.3 = (f32[32,3,2,3,1,128]{5,0,4,3,2,1:T(8,128)S(1)}, f32[32,3,2,3,1,128]{5,0,4,3,2,1:T(8,128)S(1)}, u32[]{:S(2)}, u32[]{:S(2)}) collective-permute-start(f32[32,3,2,3,1,128]{5,0,4,3,2,1:T(8,128)S(1)} %get-tuple-element.116), channel_id=1, source_target_pairs={{8,0},{16,8},{24,16},{0,24},{9,1},{17,9},{25,17},{1,25},{10,2},{18... | collective-permute-start | bytes 884744 | tf_op jit(solution)/shard_map/ppermute | solution.py:18
  113.4 6.9 %copy-start.8 = (f32[32,3,2,3,1,128]{5,0,4,3,2,1:T(8,128)}, f32[32,3,2,3,1,128]{5,0,4,3,2,1:T(8,128)S(1)}, u32[]{:S(2)}) copy-start(f32[32,3,2,3,1,128]{5,0,4,3,2,1:T(8,128)S(1)} %collective-permute-done.2) | copy-start | bytes 884740
  125.9 8.6 %collective-permute-start.5 = (f32[32,3,2,3,6,1]{0,2,5,4,3,1:T(2,128)}, f32[32,3,2,3,6,1]{0,2,5,4,3,1:T(2,128)}, u32[]{:S(2)}, u32[]{:S(2)}) collective-permute-start(f32[32,3,2,3,6,1]{0,2,5,4,3,1:T(2,128)} %copy.507), channel_id=1, source_target_pairs={{1,0},{2,1},{3,2},{4,3},{5,4},{6,5},{7,6},{0,7},{9,8},{10,9},{11,1... | collective-permute-start | bytes 41480 | tf_op jit(solution)/shard_map/ppermute | solution.py:18
  132.8 9.4 %collective-permute-start.4 = (f32[32,3,2,3,6,1]{0,2,5,4,3,1:T(2,128)}, f32[32,3,2,3,6,1]{0,2,5,4,3,1:T(2,128)}, u32[]{:S(2)}, u32[]{:S(2)}) collective-permute-start(f32[32,3,2,3,6,1]{0,2,5,4,3,1:T(2,128)} %copy.506), channel_id=1, source_target_pairs={{0,1},{1,2},{2,3},{3,4},{4,5},{5,6},{6,7},{7,0},{8,9},{9,10},{10,1... | collective-permute-start | bytes 41480 | tf_op jit(solution)/shard_map/ppermute | solution.py:15
  143.8 1.4 copy-start.54
  143.8 1.5 copy-start.72
  143.8 1.5 copy-start.9
  143.8 1.5 copy-start.11
  145.4 1.5 copy-start
  147.9 1.1 copy-start.27
  147.9 1.2 copy-start.28
  147.9 1.2 copy-start.33
  148.6 1.1 copy-start.24
  148.6 1.2 copy-start.34
  304.4 133.4 %copy-start.94 = (f32[32,32]{1,0:T(8,128)}, f32[32,32]{1,0:T(8,128)S(1)}, u32[]{:S(2)}) copy-start(f32[32,32]{1,0:T(8,128)S(1)} %get-tuple-element.76) | copy-start | bytes 12292
  307.1 2.1 copy-start.37
  307.1 2.1 copy-start.93
  307.6 2.5 copy-start.2
  307.6 2.5 copy-start.39
  307.6 2.5 copy-start.91
  307.9 5.9 %collective-permute-start.6 = (f32[32,3,2,1,4,128]{5,0,4,3,2,1:T(8,128)S(1)}, f32[32,3,2,1,4,128]{5,0,4,3,2,1:T(8,128)S(1)}, u32[]{:S(2)}, u32[]{:S(2)}) collective-permute-start(f32[32,3,2,1,4,128]{5,0,4,3,2,1:T(8,128)S(1)} %copy.482), channel_id=1, source_target_pairs={{0,32},{32,64},{64,96},{96,128},{128,160},{160,192},{192,224},{224... | collective-permute-start | bytes 1179656 | tf_op jit(solution)/shard_map/ppermute | solution.py:15
  309.1 7.5 %collective-permute-start.7 = (f32[32,3,2,1,4,128]{5,0,4,3,2,1:T(8,128)S(1)}, f32[32,3,2,1,4,128]{5,0,4,3,2,1:T(8,128)S(1)}, u32[]{:S(2)}, u32[]{:S(2)}) collective-permute-start(f32[32,3,2,1,4,128]{5,0,4,3,2,1:T(8,128)S(1)} %copy.482), channel_id=1, source_target_pairs={{32,0},{64,32},{96,64},{128,96},{160,128},{192,160},{224,192},{0,2... | collective-permute-start | bytes 1179656 | tf_op jit(solution)/shard_map/ppermute | solution.py:18
  314.0 6.2 %copy-start.85 = (f32[3,3,4,128]{3,2,0,1:T(4,128)S(1)}, f32[3,3,4,128]{3,2,0,1:T(4,128)}, u32[]{:S(2)}) copy-start(f32[3,3,4,128]{3,2,0,1:T(4,128)} %copy-done.84) | copy-start | bytes 55300
  316.7 4.2 copy-start.83
  316.7 4.2 copy-start.89
  316.7 5.1 copy-start.81
  316.7 5.1 copy-start.87
  316.7 10.0 %collective-permute-start.8 = (f32[32,3,2,3,1,128]{5,0,4,3,2,1:T(8,128)S(1)}, f32[32,3,2,3,1,128]{5,0,4,3,2,1:T(8,128)S(1)}, u32[]{:S(2)}, u32[]{:S(2)}) collective-permute-start(f32[32,3,2,3,1,128]{5,0,4,3,2,1:T(8,128)S(1)} %get-tuple-element.113), channel_id=1, source_target_pairs={{0,8},{8,16},{16,24},{24,0},{1,9},{9,17},{17,25},{25,1},{2,10},{10... | collective-permute-start | bytes 884744 | tf_op jit(solution)/shard_map/ppermute | solution.py:15
  317.7 14.3 %collective-permute-start.9 = (f32[32,3,2,3,1,128]{5,0,4,3,2,1:T(8,128)S(1)}, f32[32,3,2,3,1,128]{5,0,4,3,2,1:T(8,128)S(1)}, u32[]{:S(2)}, u32[]{:S(2)}) collective-permute-start(f32[32,3,2,3,1,128]{5,0,4,3,2,1:T(8,128)S(1)} %get-tuple-element.114), channel_id=1, source_target_pairs={{8,0},{16,8},{24,16},{0,24},{9,1},{17,9},{25,17},{1,25},{10,2},{18... | collective-permute-start | bytes 884744 | tf_op jit(solution)/shard_map/ppermute | solution.py:18
  326.7 5.3 %copy-start.4 = (f32[32,3,2,3,1,128]{5,0,4,3,2,1:T(8,128)}, f32[32,3,2,3,1,128]{5,0,4,3,2,1:T(8,128)S(1)}, u32[]{:S(2)}) copy-start(f32[32,3,2,3,1,128]{5,0,4,3,2,1:T(8,128)S(1)} %collective-permute-done.8) | copy-start | bytes 884740
  337.6 8.1 %collective-permute-start.11 = (f32[32,3,2,3,6,1]{0,2,5,4,3,1:T(2,128)}, f32[32,3,2,3,6,1]{0,2,5,4,3,1:T(2,128)}, u32[]{:S(2)}, u32[]{:S(2)}) collective-permute-start(f32[32,3,2,3,6,1]{0,2,5,4,3,1:T(2,128)} %copy.509), channel_id=1, source_target_pairs={{1,0},{2,1},{3,2},{4,3},{5,4},{6,5},{7,6},{0,7},{9,8},{10,9},{11,1... | collective-permute-start | bytes 41480 | tf_op jit(solution)/shard_map/ppermute | solution.py:18
  345.0 9.9 %collective-permute-start.10 = (f32[32,3,2,3,6,1]{0,2,5,4,3,1:T(2,128)}, f32[32,3,2,3,6,1]{0,2,5,4,3,1:T(2,128)}, u32[]{:S(2)}, u32[]{:S(2)}) collective-permute-start(f32[32,3,2,3,6,1]{0,2,5,4,3,1:T(2,128)} %copy.508), channel_id=1, source_target_pairs={{0,1},{1,2},{2,3},{3,4},{4,5},{5,6},{6,7},{7,0},{8,9},{9,10},{10,1... | collective-permute-start | bytes 41480 | tf_op jit(solution)/shard_map/ppermute | solution.py:15
  347.2 2.2 copy-start.1
  347.2 2.2 copy-start.59
  347.2 2.2 copy-start.63
  356.4 1.4 copy-start.65
  356.5 1.5 copy-start.79
  356.5 1.6 copy-start.55
  356.5 1.6 copy-start.73
  356.5 1.7 copy-start.57
  356.5 1.7 copy-start.77
  359.3 1.1 copy-start.53
  359.9 1.1 copy-start.25
  359.9 1.2 copy-start.26
  359.9 1.2 copy-start.30
  359.9 1.3 copy-start.31
  360.6 1.1 copy-start.21
  360.6 1.2 copy-start.22
  360.6 1.2 copy-start.29
  360.6 1.3 copy-start.32
  (44 other events, 39.3 us)
where the time goes:
time: 524 us; the launch traced here: 522 us
  blocking collectives  377 us (72%)
  other arithmetic  45.5 us (9%)
  local copies, waits for them, and re-layouts  39 us (7%)
  waiting for transfers between devices  31.8 us (6%)
  starting transfers between devices  19.9 us (4%)
  matrix products  7.11 us (1%)
    psum x2, blocking collectives, lanczos_step(): alpha = lax.psum(local_gram(image, basis), ('gx', 'gy', 'gz')) / row_count  148 us
    psum x2, blocking collectives, lanczos_step(): lax.psum(local_gram(residual, residual), ('gx', 'gy', 'gz')) / row_count  147 us
    psum x1, blocking collectives, local(): lax.psum(local_gram(start_block, start_block), ('gx', 'gy', 'gz'))  81.5 us
    unnamed x203, local copies, waits for them, and re-layouts  17 us
    ppermute x6, waiting for transfers between devices, extended(): lax.ppermute(lax.slice_in_dim(block, block.shape[dim] - width, None, axis...  17 us
    ppermute x6, starting transfers between devices, extended(): lax.ppermute(lax.slice_in_dim(block, 0, width, axis=dim), axis, backward)  16.3 us
    ppermute x6, waiting for transfers between devices, extended(): lax.ppermute(lax.slice_in_dim(block, 0, width, axis=dim), axis, backward)  14.8 us
    reduce_sum x42, other arithmetic, apply_hessian(): summed = summed + jnp.sum(coupling[None] * neighbour[:, None], axis=2)  12.5 us
  transfers between devices with their start and end apart: 12, of which 8 were waited for; matrix products, arithmetic and copies ran while one was open for 6% of the time, Pallas kernels for 0%

commit v1 on v0

--- a/solution.py
+++ b/solution.py
@@ -98,7 +98,7 @@
 
 
 def lanczos_step(basis, image, previous, coupling_prev, row_count):
-    alpha = lax.psum(local_gram(image, basis), ("gx", "gy", "gz")) / row_count
+    alpha = lax.psum(lax.psum(local_gram(image, basis), ("gy", "gz")), "gx") / row_count
     residual = image - combine(alpha, basis)
     if previous is not None:
         residual = residual - combine(coupling_prev.T, previous)

time: 524 us -> 759 us (1.45)
  blocking collectives: 377 us -> 612 us
    psum x2 -> x4, blocking collectives: 148 us -> 373 us  [the longest x2 274 us: lanczos_step(): lax.psum(local_gram(image, basis), ('gy', 'gz'))]
    psum x2, blocking collectives: 147 us -> 158 us  [lanczos_step(): lax.psum(local_gram(residual, residual), ('gx', 'gy', 'gz')) / row_count]
  transfers between devices with their start and end apart: 12 -> 12, of which waited for: 8 -> 8; matrix products, arithmetic and copies ran while one was open for 6% -> 4% of each run, Pallas kernels for 0% -> 0%
where the time goes in v1:
time: 759 us; the launch traced here: 758 us
  blocking collectives  612 us (81%)
  other arithmetic  45.5 us (6%)
  local copies, waits for them, and re-layouts  39 us (5%)
  waiting for transfers between devices  30.8 us (4%)
  starting transfers between devices  20.5 us (3%)
    psum x2, blocking collectives, lanczos_step(): lax.psum(local_gram(image, basis), ('gy', 'gz'))  274 us
    psum x2, blocking collectives, lanczos_step(): lax.psum(local_gram(residual, residual), ('gx', 'gy', 'gz')) / row_count  158 us
    psum x2, blocking collectives, lanczos_step(): lax.psum(lax.psum(local_gram(image, basis), ('gy', 'gz')), 'gx') / row_count  99.2 us
    psum x1, blocking collectives, local(): lax.psum(local_gram(start_block, start_block), ('gx', 'gy', 'gz'))  81.5 us
    unnamed x203, local copies, waits for them, and re-layouts  17 us
    ppermute x6, waiting for transfers between devices, extended(): lax.ppermute(lax.slice_in_dim(block, block.shape[dim] - width, None, axis...  15.8 us
  transfers between devices with their start and end apart: 12, of which 8 were waited for; matrix products, arithmetic and copies ran while one was open for 4% of the time, Pallas kernels for 0%

profile of v1, /device:TPU:1, one launch (start us, length us, event | category | flops | bytes accessed | tf_op | source)
XLA Modules:
  0.0 757.6 jit_solution(3041881404794186468)
XLA Ops:
  0.6 1.2 reshape.1549
  1.8 1.7 convolution_bitcast_fusion.2
  3.5 81.5 %psum.49 = f32[32,32]{0,1:T(8,128)S(1)} all-reduce(f32[32,32]{0,1:T(8,128)S(1)} %convolution_bitcast_fusion.2), channel_id=1, replica_groups=mesh['gx'=8,'gy'=4,'gz'=8] {'gx','gy','gz'}, use_global_device_ids=true, to_apply=%region_1.2 | all-reduce | flops 1024 | bytes 8192 | tf_op jit(solution)/shard_map/psum | solution.py:114
  85.1 2.9 cholesky.59
  88.7 0.7 fusion.44
  89.4 2.4 custom-call.7
  92.8 1.0 collective-permute-start.1
  94.2 2.5 select_reduce_fusion.13
  103.9 0.8 multiply_reduce_fusion.45
  104.8 0.8 multiply_reduce_fusion.59
  106.5 2.7 collective-permute-start.3
  109.2 0.7 slice_bitcast_fusion.9
  109.9 0.7 multiply_reduce_fusion.50
  110.6 0.9 multiply_reduce_fusion.55
  111.5 0.9 multiply_reduce_fusion.51
  112.4 1.1 collective-permute-done.2
  113.5 6.9 collective-permute-done.3
  120.4 0.7 copy-done.10
  121.3 1.8 fusion.52
  123.1 2.8 copy.507
  125.9 5.6 collective-permute-start.5
  131.5 1.3 copy.506
  132.8 1.7 multiply_reduce_fusion.36
  134.5 2.7 copy.419
  137.2 5.0 collective-permute-done.4
  142.3 1.5 copy.395
  143.8 1.4 fusion.8
  151.1 136.6 %psum.50 = f32[32,32]{0,1:T(8,128)S(1)} all-reduce(f32[32,32]{0,1:T(8,128)S(1)} %fusion.56), channel_id=1, replica_groups=mesh['gx'=8,'gy'=4,'gz'=8] {'gy','gz'}, use_global_device_ids=true, to_apply=%region_47.50 | all-reduce | flops 1024 | bytes 8192 | tf_op jit(solution)/shard_map/psum | solution.py:101
  287.7 49.5 %psum.51 = f32[32,32]{0,1:T(8,128)S(1)} all-reduce(f32[32,32]{0,1:T(8,128)S(1)} %psum.50), channel_id=1, replica_groups=mesh['gx'=8,'gy'=4,'gz'=8] {'gx'}, use_global_device_ids=true, to_apply=%region_48.51 | all-reduce | flops 1024 | bytes 8192 | tf_op jit(solution)/shard_map/psum | solution.py:101
  338.3 78.8 %psum.52 = f32[32,32]{0,1:T(8,128)S(1)} all-reduce(f32[32,32]{0,1:T(8,128)S(1)} %fusion.57), channel_id=1, replica_groups=mesh['gx'=8,'gy'=4,'gz'=8] {'gx','gy','gz'}, use_global_device_ids=true, to_apply=%region_49.52 | all-reduce | flops 1024 | bytes 8192 | tf_op jit(solution)/shard_map/psum | solution.py:105
  417.1 2.9 cholesky.70
  421.4 2.4 custom-call.8
  424.9 1.8 collective-permute-start.6
  426.8 0.8 multiply_reduce_fusion.15
  427.7 0.8 multiply_reduce_fusion.29
  429.2 2.2 collective-permute-done.6
  431.5 2.4 collective-permute-done.7
  434.0 1.4 collective-permute-start.8
  435.4 1.9 collective-permute-start.9
  437.4 0.7 multiply_reduce_fusion.20
  438.2 0.9 multiply_reduce_fusion.25
  439.0 0.9 multiply_reduce_fusion.21
  439.9 4.5 collective-permute-done.8
  444.3 5.7 collective-permute-done.9
  450.1 0.7 copy-done.6
  451.0 1.8 fusion.51
  452.9 2.8 copy.509
  455.6 3.7 collective-permute-start.11
  459.3 1.5 multiply_reduce_fusion.6
  460.8 1.3 copy.508
  462.1 1.7 collective-permute-start.10
  463.8 1.5 copy.488
  465.3 2.2 maximum_bitcast_fusion.4
  467.6 0.9 multiply_reduce_fusion.17
  468.5 3.0 collective-permute-done.10
  471.4 1.5 copy.486
  473.0 1.4 fusion.4
  480.2 137.0 %psum.53 = f32[32,32]{0,1:T(8,128)S(1)} all-reduce(f32[32,32]{0,1:T(8,128)S(1)} %fusion.59), channel_id=1, replica_groups=mesh['gx'=8,'gy'=4,'gz'=8] {'gy','gz'}, use_global_device_ids=true, to_apply=%region_80.83 | all-reduce | flops 1024 | bytes 8192 | tf_op jit(solution)/shard_map/psum | solution.py:101
  617.2 49.7 %psum.54 = f32[32,32]{0,1:T(8,128)S(1)} all-reduce(f32[32,32]{0,1:T(8,128)S(1)} %psum.53), channel_id=1, replica_groups=mesh['gx'=8,'gy'=4,'gz'=8] {'gx'}, use_global_device_ids=true, to_apply=%region_81.84 | all-reduce | flops 1024 | bytes 8192 | tf_op jit(solution)/shard_map/psum | solution.py:101
  668.6 79.2 %psum.55 = f32[32,32]{0,1:T(8,128)S(1)} all-reduce(f32[32,32]{0,1:T(8,128)S(1)} %fusion.60), channel_id=1, replica_groups=mesh['gx'=8,'gy'=4,'gz'=8] {'gx','gy','gz'}, use_global_device_ids=true, to_apply=%region_82.85 | all-reduce | flops 1024 | bytes 8192 | tf_op jit(solution)/shard_map/psum | solution.py:105
  747.9 2.9 cholesky.81
  751.5 1.3 select_bitcast_fusion
  752.7 2.4 custom-call.9
  755.9 1.0 copy.497
  (323 shorter events, 29.6 us)
Async XLA Ops:
  3.5 90.4 %copy-start.95 = (s32[16,2,1,4,128]{4,3,2,1,0:T(4,128)S(1)}, s32[16,2,1,4,128]{4,3,2,1,0:T(4,128)}, u32[]{:S(2)}) copy-start(s32[16,2,1,4,128]{4,3,2,1,0:T(4,128)} %param.8) | copy-start | bytes 196612
  88.7 5.5 copy-start.35
  92.8 12.8 %collective-permute-start = (f32[32,3,2,1,4,128]{5,0,4,3,2,1:T(8,128)S(1)}, f32[32,3,2,1,4,128]{5,0,4,3,2,1:T(8,128)S(1)}, u32[]{:S(2)}, u32[]{:S(2)}) collective-permute-start(f32[32,3,2,1,4,128]{5,0,4,3,2,1:T(8,128)S(1)} %copy.391), channel_id=1, source_target_pairs={{0,32},{32,64},{64,96},{96,128},{128,160},{160,192},{192,224},{224... | collective-permute-start | bytes 1179656 | tf_op jit(solution)/shard_map/ppermute | solution.py:15
  92.8 12.9 %collective-permute-start.1 = (f32[32,3,2,1,4,128]{5,0,4,3,2,1:T(8,128)S(1)}, f32[32,3,2,1,4,128]{5,0,4,3,2,1:T(8,128)S(1)}, u32[]{:S(2)}, u32[]{:S(2)}) collective-permute-start(f32[32,3,2,1,4,128]{5,0,4,3,2,1:T(8,128)S(1)} %copy.391), channel_id=1, source_target_pairs={{32,0},{64,32},{96,64},{128,96},{160,128},{192,160},{224,192},{0,2... | collective-permute-start | bytes 1179656 | tf_op jit(solution)/shard_map/ppermute | solution.py:18
  99.9 10.0 %copy-start.84 = (f32[3,3,4,128]{3,2,0,1:T(4,128)}, f32[3,3,4,128]{3,2,0,1:T(4,128)S(1)}, u32[]{:S(2)}) copy-start(f32[3,3,4,128]{3,2,0,1:T(4,128)S(1)} %get-tuple-element.159) | copy-start | bytes 55300
  99.9 10.7 %copy-start.82 = (f32[3,3,4,128]{3,2,0,1:T(4,128)}, f32[3,3,4,128]{3,2,0,1:T(4,128)S(1)}, u32[]{:S(2)}) copy-start(f32[3,3,4,128]{3,2,0,1:T(4,128)S(1)} %get-tuple-element.162) | copy-start | bytes 55300
  100.6 10.9 %copy-start.80 = (f32[3,3,4,128]{3,2,0,1:T(4,128)}, f32[3,3,4,128]{3,2,0,1:T(4,128)S(1)}, u32[]{:S(2)}) copy-start(f32[3,3,4,128]{3,2,0,1:T(4,128)S(1)} %get-tuple-element.194) | copy-start | bytes 55300
  102.5 8.1 %copy-start.88 = (f32[3,3,4,128]{3,2,0,1:T(4,128)}, f32[3,3,4,128]{3,2,0,1:T(4,128)S(1)}, u32[]{:S(2)}) copy-start(f32[3,3,4,128]{3,2,0,1:T(4,128)S(1)} %get-tuple-element.190) | copy-start | bytes 55300
  102.5 9.0 %copy-start.86 = (f32[3,3,4,128]{3,2,0,1:T(4,128)}, f32[3,3,4,128]{3,2,0,1:T(4,128)S(1)}, u32[]{:S(2)}) copy-start(f32[3,3,4,128]{3,2,0,1:T(4,128)S(1)} %get-tuple-element.189) | copy-start | bytes 55300
  103.8 1.8 copy-start.90
  103.8 1.8 copy-start.92
  103.9 1.9 copy-start.36
  104.8 1.1 copy-start.38
  105.8 7.6 %collective-permute-start.2 = (f32[32,3,2,3,1,128]{5,0,4,3,2,1:T(8,128)S(1)}, f32[32,3,2,3,1,128]{5,0,4,3,2,1:T(8,128)S(1)}, u32[]{:S(2)}, u32[]{:S(2)}) collective-permute-start(f32[32,3,2,3,1,128]{5,0,4,3,2,1:T(8,128)S(1)} %get-tuple-element.115), channel_id=1, source_target_pairs={{0,8},{8,16},{16,24},{24,0},{1,9},{9,17},{17,25},{25,1},{2,10},{10... | collective-permute-start | bytes 884744 | tf_op jit(solution)/shard_map/ppermute | solution.py:15
  106.5 13.9 %collective-permute-start.3 = (f32[32,3,2,3,1,128]{5,0,4,3,2,1:T(8,128)S(1)}, f32[32,3,2,3,1,128]{5,0,4,3,2,1:T(8,128)S(1)}, u32[]{:S(2)}, u32[]{:S(2)}) collective-permute-start(f32[32,3,2,3,1,128]{5,0,4,3,2,1:T(8,128)S(1)} %get-tuple-element.116), channel_id=1, source_target_pairs={{8,0},{16,8},{24,16},{0,24},{9,1},{17,9},{25,17},{1,25},{10,2},{18... | collective-permute-start | bytes 884744 | tf_op jit(solution)/shard_map/ppermute | solution.py:18
  113.4 6.9 copy-start.8
  125.9 8.6 %collective-permute-start.5 = (f32[32,3,2,3,6,1]{0,2,5,4,3,1:T(2,128)}, f32[32,3,2,3,6,1]{0,2,5,4,3,1:T(2,128)}, u32[]{:S(2)}, u32[]{:S(2)}) collective-permute-start(f32[32,3,2,3,6,1]{0,2,5,4,3,1:T(2,128)} %copy.507), channel_id=1, source_target_pairs={{1,0},{2,1},{3,2},{4,3},{5,4},{6,5},{7,6},{0,7},{9,8},{10,9},{11,1... | collective-permute-start | bytes 41480 | tf_op jit(solution)/shard_map/ppermute | solution.py:18
  132.8 9.4 %collective-permute-start.4 = (f32[32,3,2,3,6,1]{0,2,5,4,3,1:T(2,128)}, f32[32,3,2,3,6,1]{0,2,5,4,3,1:T(2,128)}, u32[]{:S(2)}, u32[]{:S(2)}) collective-permute-start(f32[32,3,2,3,6,1]{0,2,5,4,3,1:T(2,128)} %copy.506), channel_id=1, source_target_pairs={{0,1},{1,2},{2,3},{3,4},{4,5},{5,6},{6,7},{7,0},{8,9},{9,10},{10,1... | collective-permute-start | bytes 41480 | tf_op jit(solution)/shard_map/ppermute | solution.py:15
  143.8 1.4 copy-start.54
  143.8 1.5 copy-start.72
  143.8 1.5 copy-start.9
  143.8 1.5 copy-start.11
  145.4 1.5 copy-start
  147.9 1.1 copy-start.27
  147.9 1.2 copy-start.28
  148.0 1.2 copy-start.33
  148.7 1.1 copy-start.24
  148.7 1.2 copy-start.34
  421.4 246.0 %copy-start.94 = (f32[32,32]{1,0:T(8,128)}, f32[32,32]{1,0:T(8,128)S(1)}, u32[]{:S(2)}) copy-start(f32[32,32]{1,0:T(8,128)S(1)} %get-tuple-element.76) | copy-start | bytes 12292
  424.1 2.7 copy-start.37
  424.1 2.7 copy-start.93
  424.6 3.1 copy-start.2
  424.6 3.1 copy-start.39
  424.6 3.1 copy-start.91
  424.9 6.5 collective-permute-start.6
  426.7 7.2 collective-permute-start.7
  431.5 5.9 copy-start.85
  433.9 4.2 copy-start.83
  433.9 4.2 copy-start.89
  433.9 5.1 copy-start.81
  434.0 5.1 copy-start.87
  434.0 10.3 %collective-permute-start.8 = (f32[32,3,2,3,1,128]{5,0,4,3,2,1:T(8,128)S(1)}, f32[32,3,2,3,1,128]{5,0,4,3,2,1:T(8,128)S(1)}, u32[]{:S(2)}, u32[]{:S(2)}) collective-permute-start(f32[32,3,2,3,1,128]{5,0,4,3,2,1:T(8,128)S(1)} %get-tuple-element.113), channel_id=1, source_target_pairs={{0,8},{8,16},{16,24},{24,0},{1,9},{9,17},{17,25},{25,1},{2,10},{10... | collective-permute-start | bytes 884744 | tf_op jit(solution)/shard_map/ppermute | solution.py:15
  435.4 14.7 %collective-permute-start.9 = (f32[32,3,2,3,1,128]{5,0,4,3,2,1:T(8,128)S(1)}, f32[32,3,2,3,1,128]{5,0,4,3,2,1:T(8,128)S(1)}, u32[]{:S(2)}, u32[]{:S(2)}) collective-permute-start(f32[32,3,2,3,1,128]{5,0,4,3,2,1:T(8,128)S(1)} %get-tuple-element.114), channel_id=1, source_target_pairs={{8,0},{16,8},{24,16},{0,24},{9,1},{17,9},{25,17},{1,25},{10,2},{18... | collective-permute-start | bytes 884744 | tf_op jit(solution)/shard_map/ppermute | solution.py:18
  444.3 5.7 copy-start.4
  455.6 8.1 %collective-permute-start.11 = (f32[32,3,2,3,6,1]{0,2,5,4,3,1:T(2,128)}, f32[32,3,2,3,6,1]{0,2,5,4,3,1:T(2,128)}, u32[]{:S(2)}, u32[]{:S(2)}) collective-permute-start(f32[32,3,2,3,6,1]{0,2,5,4,3,1:T(2,128)} %copy.509), channel_id=1, source_target_pairs={{1,0},{2,1},{3,2},{4,3},{5,4},{6,5},{7,6},{0,7},{9,8},{10,9},{11,1... | collective-permute-start | bytes 41480 | tf_op jit(solution)/shard_map/ppermute | solution.py:18
  462.1 9.4 %collective-permute-start.10 = (f32[32,3,2,3,6,1]{0,2,5,4,3,1:T(2,128)}, f32[32,3,2,3,6,1]{0,2,5,4,3,1:T(2,128)}, u32[]{:S(2)}, u32[]{:S(2)}) collective-permute-start(f32[32,3,2,3,6,1]{0,2,5,4,3,1:T(2,128)} %copy.508), channel_id=1, source_target_pairs={{0,1},{1,2},{2,3},{3,4},{4,5},{5,6},{6,7},{7,0},{8,9},{9,10},{10,1... | collective-permute-start | bytes 41480 | tf_op jit(solution)/shard_map/ppermute | solution.py:15
  465.3 2.2 copy-start.1
  465.3 2.2 copy-start.59
  465.3 2.2 copy-start.63
  473.0 1.4 copy-start.65
  473.0 1.5 copy-start.79
  473.0 1.6 copy-start.55
  473.0 1.6 copy-start.73
  473.0 1.7 copy-start.57
  473.0 1.7 copy-start.77
  475.8 1.1 copy-start.53
  476.4 1.1 copy-start.25
  476.4 1.2 copy-start.26
  476.4 1.2 copy-start.30
  476.4 1.3 copy-start.31
  477.1 1.1 copy-start.21
  477.1 1.2 copy-start.22
  477.1 1.2 copy-start.29
  477.1 1.3 copy-start.32
  (44 other events, 39.3 us)
